TPU v7x, 512 devices: a whole 4x8x8 slice. The times are simulated.
512 devices in a mesh: lower: 16 (over y, core), upper: 8 (over z), depth: 4 (over x).
Axes of the slice: x: 4, y: 8, z: 8, core: 2. Of those that a mesh axis runs over, the one named last changes fastest.
Arguments:
- lower_vectors: bfloat16 [4, 32768, 2048], P('depth', 'lower', 'upper'), may hold values from -0.0234375 to 0.0234375
- upper_vectors: bfloat16 [4, 32768, 3072], P('depth', 'lower', 'upper'), may hold values from -6 to 6
- energy_lower: float32 [2048], P(('lower', 'depth')), may hold values from 0 to 0.5
- energy_upper: float32 [3072], P('upper'), may hold values from 1 to 2
- sym_lower: int32 [2048], P(('lower', 'depth')), may hold values from 0 to 3
- sym_upper: int32 [3072], P('upper'), may hold values from 0 to 3
- j_lower: int32 [2048], P(('lower', 'depth')), may hold values from 0 to 2
- j_upper: int32 [3072], P('upper'), may hold values from 0 to 2
Outputs:
- einstein: float32 [2048, 3072], P(('lower', 'depth'), 'upper')
All inputs are finite; a program needn't handle non-finite values.
Results may differ from a plain program's by a relative error of at most 0.0003.
Values may be sent and summed in bfloat16 or wider, within the bound.
A program may use at most 64 MiB of HBM per device.

v0:
```python
import jax
import jax.numpy as jnp
from jax import lax
from jax.sharding import PartitionSpec as P


def local(
    lower_vectors, upper_vectors, energy_lower, energy_upper, sym_lower, sym_upper, j_lower, j_upper
):
    lower_rows = lower_vectors[0]
    upper_rows = upper_vectors[0]
    partial_terms = lax.dot_general(
        lax.all_gather(lower_rows, "upper", axis=1, tiled=True),
        upper_rows,
        (((0,), (0,)), ((), ())),
        preferred_element_type=jnp.float32,
    )
    moments = lax.psum_scatter(partial_terms, ("lower", "depth"), scatter_dimension=0, tiled=True)
    parity = sym_lower % 2
    sym_rule = sym_upper[None, :] - sym_lower[:, None] == (1 - 2 * parity)[:, None]
    j_rule = jnp.abs(j_upper[None, :] - j_lower[:, None]) <= 1
    allowed = jnp.logical_and(sym_rule, j_rule)
    frequency = energy_upper[None, :] - energy_lower[:, None]
    weight_upper = (2 * j_upper + 1).astype(jnp.float32)
    value = frequency * frequency * frequency * (moments * moments) / weight_upper[None, :]
    return jnp.where(allowed, value, jnp.zeros_like(value))


def solution(mesh):
    return jax.shard_map(
        local,
        mesh=mesh,
        in_specs=(
            P("depth", "lower", "upper"),
            P("depth", "lower", "upper"),
            P(("lower", "depth")),
            P("upper"),
            P(("lower", "depth")),
            P("upper"),
            P(("lower", "depth")),
            P("upper"),
        ),
        out_specs=P(("lower", "depth"), "upper"),
        check_vma=False,
    )
```

profile of v0, /device:TPU:16, one launch (start us, length us, event | category | flops | bytes accessed | tf_op | source)
XLA Modules:
  0.0 283.6 jit_solution(9405413848341315890)
XLA Ops:
  6.5 0.0 copy-start
  6.5 0.0 all-gather.3.cloned.1.call-start
  6.5 0.7 all-gather.3.cloned.1.call-update
  7.3 0.0 reduce-scatter.2.cloned.1.call-start
  7.3 110.6 %all-gather.3.cloned.1.call-done = bf16[1,2048,2048]{2,1,0:T(8,128)(2,1)} async-done(((bf16[1,2048,256]{2,1,0:T(8,128)(2,1)}), bf16[1,2048,2048]{2,1,0:T(8,128)(2,1)}) %all-gather.3.cloned.1.call-update) | async-done | bytes 8388624 | tf_op jit(solution)/shard_map/all_gather | solution.py:13
  117.9 0.0 copy-done
  117.9 8.7 %fusion = f32[2048,384]{1,0:T(8,128)} fusion(bf16[1,2048,2048]{2,1,0:T(8,128)(2,1)} %all-gather.3.cloned.1.call-done, bf16[1,2048,384]{2,1,0:T(8,128)(2,1)S(1)} %copy-done), kind=kOutput, calls=%fused_computation | convolution fusion | flops 3221225472 | bytes 13107200 | tf_op jit(solution)/shard_map/dot_general | solution.py:12
  126.6 0.0 copy-start.6
  126.6 0.0 copy-start.1
  126.6 0.0 copy-start.2
  126.6 0.0 copy-start.3
  126.7 0.0 copy-start.4
  126.7 0.0 copy-start.5
  126.7 0.0 reduce-scatter.2.cloned.1.call-update
  126.7 0.6 copy-done.6
  127.3 0.0 copy-done.1
  127.3 147.9 %reduce-scatter.2.cloned.1.call-done = f32[32,384]{1,0:T(8,128)} async-done(((f32[2048,384]{1,0:T(8,128)}), f32[32,384]{1,0:T(8,128)}) %reduce-scatter.2.cloned.1.call-update) | async-done | bytes 49168 | tf_op jit(solution)/shard_map/reduce_scatter | solution.py:18
  275.2 0.0 copy-done.2
  275.2 0.0 copy-done.3
  275.2 0.0 copy-done.4
  275.2 0.0 copy-done.5
  275.2 1.5 fusion.5
  (2 shorter events, 0.0 us)
Async XLA Ops:
  6.5 111.4 %copy-start = (bf16[1,2048,384]{2,1,0:T(8,128)(2,1)S(1)}, bf16[1,2048,384]{2,1,0:T(8,128)(2,1)}, u32[]{:S(2)}) copy-start(bf16[1,2048,384]{2,1,0:T(8,128)(2,1)} %param.9) | copy-start | bytes 4718596
  6.5 111.4 %all-gather.3.cloned.1.call-start = ((), (), s32[]{:S(2)}) async-start(), calls=%async_computation.2 | async-start | bytes 9437184 | tf_op jit(solution)/shard_map/all_gather | solution.py:13
  7.3 268.0 %reduce-scatter.2.cloned.1.call-start = ((), (), s32[]{:S(2)}) async-start(), calls=%async_computation.1 | async-start | bytes 3194880 | tf_op jit(solution)/shard_map/reduce_scatter | solution.py:18
  126.6 0.7 copy-start.6
  126.6 0.7 copy-start.1
  126.6 148.6 %copy-start.2 = (f32[384]{0:T(512)S(1)}, f32[384]{0:T(512)}, u32[]{:S(2)}) copy-start(f32[384]{0:T(512)} %param.11) | copy-start | bytes 4612
  126.6 148.6 %copy-start.3 = (s32[384]{0:T(512)S(1)}, s32[384]{0:T(512)}, u32[]{:S(2)}) copy-start(s32[384]{0:T(512)} %param.13) | copy-start | bytes 4612
  126.7 148.6 %copy-start.4 = (f32[32]{0:T(128)S(1)}, f32[32]{0:T(128)}, u32[]{:S(2)}) copy-start(f32[32]{0:T(128)} %param.10) | copy-start | bytes 388
  126.7 148.6 %copy-start.5 = (s32[32]{0:T(128)S(1)}, s32[32]{0:T(128)}, u32[]{:S(2)}) copy-start(s32[32]{0:T(128)} %param.14) | copy-start | bytes 388
Sparse Core Ops, SparseCore 0:
  9.4 108.5 all-gather.2
  126.8 148.3 reduce-scatter.1
where the time goes:
time: 284 us
  waiting for transfers between devices  259 us (91%)
  between operations  13.4 us (5%)
  matrix products  8.69 us (3%)
    reduce_scatter x1, waiting for transfers between devices, local(): lax.psum_scatter(partial_terms, ('lower', 'depth'), scatter_dimension=0,...  148 us
    all_gather x1, waiting for transfers between devices, local(): lax.all_gather(lower_rows, 'upper', axis=1, tiled=True)  111 us
    dot_general x1, matrix products, local(): lax.dot_general(lax.all_gather(lower_rows, 'upper', axis=1, tiled=True),...  8.69 us
  transfers between devices with their start and end apart: 2, of which 2 were waited for; matrix products, arithmetic and copies ran while one was open for 0% of the time, Pallas kernels for 0%

commit v1 on v0

--- a/solution.py
+++ b/solution.py
@@ -10,7 +10,9 @@
     lower_rows = lower_vectors[0]
     upper_rows = upper_vectors[0]
     partial_terms = lax.dot_general(
-        lax.all_gather(lower_rows, "upper", axis=1, tiled=True),
+        jnp.concatenate(
+            lax.all_to_all(jnp.stack([lower_rows] * lax.axis_size("upper")), "upper", 0, 0), axis=1
+        ),
         upper_rows,
         (((0,), (0,)), ((), ())),
         preferred_element_type=jnp.float32,

time: 284 us -> 367 us (1.29)
  blocking collectives: 0 us -> 196 us
  waiting for transfers between devices: 259 us -> 146 us
    all_to_all x0 -> x1, blocking collectives: none -> 196 us  [local(): lax.all_to_all(jnp.stack([lower_rows] * lax.axis_size('upper')), 'upper',...]
    all_gather x1 -> x0, waiting for transfers between devices: 111 us -> none  [local(): lax.all_gather(lower_rows, 'upper', axis=1, tiled=True)]
  transfers between devices with their start and end apart: 2 -> 1, of which waited for: 2 -> 1; matrix products, arithmetic and copies ran while one was open for 0% -> 0% of each run, Pallas kernels for 0% -> 0%
where the time goes in v1:
time: 367 us; the launch traced here: 366 us
  blocking collectives  196 us (53%)
  waiting for transfers between devices  146 us (40%)
  between operations  13.4 us (4%)
  matrix products  6.3 us (2%)
    all_to_all x1, blocking collectives, local(): lax.all_to_all(jnp.stack([lower_rows] * lax.axis_size('upper')), 'upper',...  196 us
    reduce_scatter x1, waiting for transfers between devices, local(): lax.psum_scatter(partial_terms, ('lower', 'depth'), scatter_dimension=0,...  146 us
  transfers between devices with their start and end apart: 1, of which 1 were waited for; matrix products, arithmetic and copies ran while one was open for 0% of the time, Pallas kernels for 0%

profile of v1, /device:TPU:16, one launch (start us, length us, event | category | flops | bytes accessed | tf_op | source)
XLA Modules:
  0.0 366.4 jit_solution(10670705558311870633)
XLA Ops:
  6.5 0.0 copy-start
  6.5 0.0 reduce-scatter.2.cloned.1.call-start
  6.5 1.6 copy.9
  8.1 1.1 stack.3
  9.2 196.1 %all_to_all.5 = bf16[8,2048,256]{1,2,0:T(8,128)(2,1)S(1)} all-to-all(bf16[8,2048,256]{1,2,0:T(8,128)(2,1)S(1)} %stack.3), channel_id=1, replica_groups=mesh['lower'=16,'upper'=8,'depth'=4] {'upper'}, dimensions={0} | all-to-all | bytes 16777216 | tf_op jit(solution)/shard_map/all_to_all | solution.py:14
  205.3 0.0 copy-done
  205.3 6.3 %fusion = f32[2048,384]{1,0:T(8,128)} fusion(bf16[2048,2048]{0,1:T(8,128)(2,1)S(1)} %bitcast.8, bf16[1,2048,384]{2,1,0:T(8,128)(2,1)S(1)} %copy-done), kind=kOutput, calls=%fused_computation | convolution fusion | flops 3221225472 | bytes 13107200 | tf_op jit(solution)/shard_map/dot_general | solution.py:12
  211.6 0.0 copy-start.6
  211.7 0.0 copy-start.1
  211.7 0.0 copy-start.2
  211.7 0.0 copy-start.3
  211.7 0.0 copy-start.4
  211.7 0.0 copy-start.5
  211.7 0.0 reduce-scatter.2.cloned.1.call-update
  211.7 0.6 copy-done.6
  212.3 0.0 copy-done.1
  212.4 145.6 %reduce-scatter.2.cloned.1.call-done = f32[32,384]{1,0:T(8,128)} async-done(((f32[2048,384]{1,0:T(8,128)}), f32[32,384]{1,0:T(8,128)}) %reduce-scatter.2.cloned.1.call-update) | async-done | bytes 49168 | tf_op jit(solution)/shard_map/reduce_scatter | solution.py:20
  358.0 0.0 copy-done.2
  358.0 0.0 copy-done.3
  358.0 0.0 copy-done.4
  358.0 0.0 copy-done.5
  358.0 1.5 fusion.4
  (2 shorter events, 0.0 us)
Async XLA Ops:
  6.5 198.8 %copy-start = (bf16[1,2048,384]{2,1,0:T(8,128)(2,1)S(1)}, bf16[1,2048,384]{2,1,0:T(8,128)(2,1)}, u32[]{:S(2)}) copy-start(bf16[1,2048,384]{2,1,0:T(8,128)(2,1)} %param.9) | copy-start | bytes 4718596
  6.5 351.4 %reduce-scatter.2.cloned.1.call-start = ((), (), s32[]{:S(2)}) async-start(), calls=%async_computation.2 | async-start | bytes 3194880 | tf_op jit(solution)/shard_map/reduce_scatter | solution.py:20
  211.6 0.7 copy-start.6
  211.7 0.7 copy-start.1
  211.7 146.3 %copy-start.2 = (f32[384]{0:T(512)S(1)}, f32[384]{0:T(512)}, u32[]{:S(2)}) copy-start(f32[384]{0:T(512)} %param.11) | copy-start | bytes 4612
  211.7 146.3 %copy-start.3 = (s32[384]{0:T(512)S(1)}, s32[384]{0:T(512)}, u32[]{:S(2)}) copy-start(s32[384]{0:T(512)} %param.13) | copy-start | bytes 4612
  211.7 146.3 %copy-start.4 = (f32[32]{0:T(128)S(1)}, f32[32]{0:T(128)}, u32[]{:S(2)}) copy-start(f32[32]{0:T(128)} %param.10) | copy-start | bytes 388
  211.7 146.3 %copy-start.5 = (s32[32]{0:T(128)S(1)}, s32[32]{0:T(128)}, u32[]{:S(2)}) copy-start(s32[32]{0:T(128)} %param.14) | copy-start | bytes 388
Sparse Core Ops, SparseCore 0:
  211.8 146.1 reduce-scatter.1
